TPU v7x, 32 devices: a whole 2x2x4 slice. The times are simulated.
32 devices in a mesh: gx: 2 (over x), gy: 4 (over y, core), gz: 4 (over z).
Axes of the slice: x: 2, y: 2, z: 4, core: 2. Of those that a mesh axis runs over, the one named last changes fastest.
Arguments:
- seed_cotangent: bfloat16 [2, 4, 4, 112, 2048], P('gx', 'gy', 'gz'), may hold values from -6 to 6
- trace_operator: bfloat16 [2, 4, 4, 2048, 2048], P('gx', 'gy', 'gz'), may hold values from -0.125 to 0.125
- face_matrices: bfloat16 [2, 4, 4, 6, 340, 340], P('gx', 'gy', 'gz'), may hold values from -0.3125 to 0.3125
- saved_traces: bfloat16 [2, 4, 4, 3, 112, 2048], P('gx', 'gy', 'gz'), may hold values from -6 to 6
- edge_flags: int32 [2, 4, 4, 6], P('gx', 'gy', 'gz'), may hold values 0 or 1
- node_map: int32 [2, 4, 4, 6, 340], P('gx', 'gy', 'gz'), may hold values from 0 to 339, each once within a row
Outputs:
- adjoint_traces: bfloat16 [2, 4, 4, 112, 2048], P('gx', 'gy', 'gz')
- face_gradient: bfloat16 [2, 4, 4, 6, 340, 340], P('gx', 'gy', 'gz')
Inputs may be any that keep to these rules, and one draw needn't show every extreme that they name: Each row node_map[.., k, :] names every face node once.
All inputs are finite; a program needn't handle non-finite values. No bound on the sum of `edge_flags` on one device may be relied on, other than what follows from the above.
Results may differ from a plain program's by a relative error of at most 0.0085.
Values may be sent and summed in bfloat16 or wider, within the bound.
A program may use at most 64 MiB of HBM per device.

v0:
```python
import functools
import math

import jax
import jax.numpy as jnp
from jax import lax
from jax.experimental import pallas as pl
from jax.experimental.pallas import tpu as pltpu
from jax.sharding import PartitionSpec as P

LANES = 128
BLOCK = 256
AXES = ("gx", "gy", "gz")


def up(value, step):
    return -(-value // step) * step


def kernel(
    width, seed_hbm, op_hbm, m_hbm, saved_hbm, map_hbm, flag_ref, out_ref, grad_ref,
    seed_v, op_v, m_v, saved_v, map_v, sel_v, w_v, send_v, recv_v, inp_v, mapped_v, packed_v,
    hid_v, acc_v, st_v, stb_v, g_v,
    in_sem, send_sem, recv_sem,
):
    columns, trace = seed_v.shape
    sweeps = saved_v.shape[0]
    pad = up(width, LANES)
    span = 6 * width
    scale = 1.0 / math.sqrt(columns)
    x_end = up(2 * width, BLOCK)
    z_start = (4 * width) // BLOCK * BLOCK
    chunks = ((z_start, trace), (0, x_end), (x_end, z_start))
    order = ((4, 5), (0, 1), (2, 3))

    where = [lax.axis_index(name) for name in AXES]
    has = []
    for axis, name in enumerate(AXES):
        has.append(where[axis] > 0)
        has.append(where[axis] < lax.axis_size(name) - 1)

    def peer(face):
        return {AXES[face // 2]: where[face // 2] + (1 if face % 2 else -1)}

    def span_of(face):
        base = face * width // LANES * LANES
        shift = face * width - base
        return base, shift, up(shift + width, LANES)

    barrier = pltpu.get_barrier_semaphore()
    count = 0
    for face in range(6):
        @pl.when(has[face])
        def _(face=face):
            pl.semaphore_signal(
                barrier, inc=1, device_id=peer(face), device_id_type=pl.DeviceIdType.MESH
            )
        count = count + has[face].astype(jnp.int32)

    seed_in = pltpu.make_async_copy(seed_hbm, seed_v, in_sem.at[0])
    seed_in.start()
    op_in = []
    for number, (start, stop) in enumerate(chunks):
        copy = pltpu.make_async_copy(
            op_hbm.at[:, start:stop], op_v.at[:, start:stop], in_sem.at[1 + number]
        )
        copy.start()
        op_in.append(copy)
    map_in = pltpu.make_async_copy(map_hbm, map_v, in_sem.at[6])
    map_in.start()
    m_in = pltpu.make_async_copy(m_hbm, m_v, in_sem.at[4])
    m_in.start()
    saved_in = pltpu.make_async_copy(saved_hbm, saved_v, in_sem.at[5])
    saved_in.start()

    for face in range(6):
        @pl.when(jnp.logical_not(has[face]))
        def _(face=face):
            for sweep in range(sweeps):
                recv_v[sweep, face] = jnp.zeros((columns, pad), jnp.bfloat16)

    def remote(sweep, face):
        return pltpu.make_async_remote_copy(
            src_ref=send_v.at[sweep, face],
            dst_ref=recv_v.at[sweep, face ^ 1],
            send_sem=send_sem.at[sweep, face],
            recv_sem=recv_sem.at[sweep, face ^ 1],
            device_id=peer(face),
            device_id_type=pl.DeviceIdType.MESH,
        )

    def arrival(sweep, face):
        return pltpu.make_async_remote_copy(
            src_ref=send_v.at[sweep, face],
            dst_ref=recv_v.at[sweep, face],
            send_sem=send_sem.at[sweep, face],
            recv_sem=recv_sem.at[sweep, face],
            device_id=peer(face),
            device_id_type=pl.DeviceIdType.MESH,
        )

    def take_face(value, shift):
        if shift:
            value = pltpu.roll(value, value.shape[1] - shift, 1)
        return value[:, :pad].astype(jnp.bfloat16)

    def dot(left, right):
        return jnp.dot(left, right, preferred_element_type=jnp.float32)

    def emit(sweep, number):
        for face in order[number]:
            base, shift, extent = span_of(face)
            send_v[sweep, face] = take_face(hid_v[:, base : base + extent], shift)
        for face in order[number]:
            @pl.when(has[face])
            def _(face=face):
                remote(sweep, face).start()

    def absorb(sweep, number):
        for face in order[number]:
            @pl.when(has[face])
            def _(face=face):
                arrival(sweep, face).wait_recv()

        for face in order[number]:
            inputs = lax.select(flag_ref[face] == 1, send_v[sweep, face], recv_v[sweep, face])
            inp_v[sweep, face] = inputs
            fresh = dot(inputs, w_v[face])
            base, shift, extent = span_of(face)
            if extent > pad:
                fresh = jnp.concatenate(
                    [fresh, jnp.zeros((columns, extent - pad), jnp.float32)], axis=1
                )
            if shift:
                fresh = pltpu.roll(fresh, shift, 1)
            st_v[:, base : base + extent] += fresh

    def map_inputs(sweep, faces=range(6)):
        for face in faces:
            mapped_v[face, sweep * columns : (sweep + 1) * columns, :] = dot(
                inp_v[sweep, face], sel_v[face]
            ).astype(jnp.bfloat16)

    def outer(face, start, stop):
        return lax.dot_general(
            mapped_v[face, start:stop, :],
            packed_v[face, start:stop, :],
            (((0,), (0,)), ((), ())),
            preferred_element_type=jnp.float32,
        )

    seed_in.wait()
    for sweep in range(sweeps):
        last = sweep == sweeps - 1
        for number, (start, stop) in enumerate(chunks):
            if sweep == 0:
                op_in[number].wait()
                hidden = dot(seed_v[...], op_v[:, start:stop])
            else:
                hidden = acc_v[:, start:stop] + dot(stb_v[:, 0:x_end], op_v[0:x_end, start:stop])
            hid_v[:, start:stop] = hidden
            if sweep == 0 and number == 0:
                pl.semaphore_wait(barrier, count)
            emit(sweep, number)

        if sweep == 0:
            map_in.wait()
            rows = lax.broadcasted_iota(jnp.int32, (pad, width), 0).astype(jnp.int16)
            lane = lax.broadcasted_iota(jnp.int32, (1, width), 1)
            for face in range(6):
                flag = (flag_ref[face] == 1).astype(jnp.int32)
                row = map_v[face]
                row = row + (lane - row) * flag
                sel_v[face, :, width:pad] = jnp.zeros((pad, pad - width), jnp.bfloat16)
                sel_v[face, :, 0:width] = jnp.where(
                    rows == row.astype(jnp.int16), jnp.bfloat16(1.0), jnp.bfloat16(0.0)
                )
                w_v[face, :, width:pad] = jnp.zeros((pad, pad - width), jnp.bfloat16)
            m_in.wait()
            for face in range(6):
                w_v[face, :, 0:width] = dot(sel_v[face, :, 0:width], m_v[face]).astype(jnp.bfloat16)
        if sweep == 1:
            saved_in.wait()
            for face in range(6):
                base, shift, extent = span_of(face)
                for step in range(sweeps):
                    packed_v[face, step * columns : (step + 1) * columns, :] = take_face(
                        saved_v[sweeps - 1 - step, :, base : base + extent].astype(jnp.float32), shift
                    )
        if sweep >= 1:
            map_inputs(sweep - 1)
        if last:
            for face in range(6):
                g_v[face] = outer(face, 0, sweep * columns)

        st_v[...] = seed_v[...].astype(jnp.float32)
        tail = hid_v[:, trace - LANES : trace].astype(jnp.bfloat16).astype(jnp.float32)
        place = lax.broadcasted_iota(jnp.int32, (columns, LANES), 1) + (trace - LANES)
        st_v[:, trace - LANES : trace] += jnp.where(place >= span, tail, 0.0)
        for number in (2, 0, 1):
            absorb(sweep, number)
            start, stop = chunks[number]
            if last:
                map_inputs(sweep, order[number])
                for face in order[number]:
                    total = g_v[face] + outer(face, sweep * columns, (sweep + 1) * columns)
                    grad_ref[face] = (total * scale).astype(jnp.bfloat16)[0:width, 0:width]
            else:
                stb_v[:, start:stop] = st_v[:, start:stop].astype(jnp.bfloat16)
                if number == 2:
                    acc_v[...] = dot(stb_v[:, start:stop], op_v[start:stop, :])
                elif number == 0:
                    acc_v[...] += dot(stb_v[:, start:stop], op_v[start:stop, :])

    out_ref[...] = st_v[...].astype(jnp.bfloat16)
    for sweep in range(sweeps):
        for face in range(6):
            @pl.when(has[face])
            def _(face=face, sweep=sweep):
                remote(sweep, face).wait_send()


def local(seed_cotangent, trace_operator, face_matrices, saved_traces, edge_flags, node_map):
    seed, operator, matrices, stored, flags, mapping = (
        array.reshape(array.shape[3:])
        for array in (
            seed_cotangent, trace_operator, face_matrices, saved_traces, edge_flags, node_map
        )
    )
    width = matrices.shape[-1]
    sweeps, columns, trace = stored.shape
    pad = up(width, LANES)
    bf16, f32 = jnp.bfloat16, jnp.float32
    anywhere = pl.BlockSpec(memory_space=pltpu.HBM)
    resident = pl.BlockSpec(memory_space=pltpu.VMEM)
    adjoint, gradient = pl.pallas_call(
        functools.partial(kernel, width),
        out_shape=(
            jax.ShapeDtypeStruct(seed.shape, bf16),
            jax.ShapeDtypeStruct(matrices.shape, bf16),
        ),
        in_specs=[anywhere] * 5
        + [pl.BlockSpec(memory_space=pltpu.SMEM)],
        out_specs=(resident, resident),
        scratch_shapes=[
            pltpu.VMEM(seed.shape, bf16),
            pltpu.VMEM(operator.shape, bf16),
            pltpu.VMEM(matrices.shape, bf16),
            pltpu.VMEM(stored.shape, bf16),
            pltpu.VMEM((6, 1, width), jnp.int32),
            pltpu.VMEM((6, pad, pad), bf16),
            pltpu.VMEM((6, pad, pad), bf16),
            pltpu.VMEM((sweeps, 6, columns, pad), bf16),
            pltpu.VMEM((sweeps, 6, columns, pad), bf16),
            pltpu.VMEM((sweeps, 6, columns, pad), bf16),
            pltpu.VMEM((6, sweeps * columns, pad), bf16),
            pltpu.VMEM((6, sweeps * columns, pad), bf16),
            pltpu.VMEM(seed.shape, f32),
            pltpu.VMEM(seed.shape, f32),
            pltpu.VMEM(seed.shape, f32),
            pltpu.VMEM(seed.shape, bf16),
            pltpu.VMEM((6, pad, pad), f32),
            pltpu.SemaphoreType.DMA((7,)),
            pltpu.SemaphoreType.DMA((sweeps, 6)),
            pltpu.SemaphoreType.DMA((sweeps, 6)),
        ],
        compiler_params=pltpu.CompilerParams(
            collective_id=0, has_side_effects=True, vmem_limit_bytes=40 * 1024 * 1024
        ),
    )(*(pltpu.with_memory_space_constraint(array, pltpu.HBM) for array in (seed, operator, matrices, stored, mapping[:, None, :], flags)))
    return adjoint[None, None, None], gradient[None, None, None]


def solution(mesh):
    return jax.shard_map(
        local,
        mesh=mesh,
        in_specs=(
            P("gx", "gy", "gz", None, None),
            P("gx", "gy", "gz", None, None),
            P("gx", "gy", "gz", None, None, None),
            P("gx", "gy", "gz", None, None, None),
            P("gx", "gy", "gz", None),
            P("gx", "gy", "gz", None, None),
        ),
        out_specs=(P("gx", "gy", "gz", None, None), P("gx", "gy", "gz", None, None, None)),
        check_vma=False,
    )
```

profile of v0, /device:TPU:1, one launch (start us, length us, event | category | flops | bytes accessed | tf_op | source)
XLA Modules:
  0.0 27.0 jit_solution(16506464349434799333)
XLA Ops:
  0.6 24.4 %shard_map.77 = (bf16[112,2048]{1,0:T(8,128)(2,1)S(1)}, bf16[6,340,340]{2,1,0:T(8,128)(2,1)S(1)}) custom-call(bf16[112,2048]{1,0:T(8,128)(2,1)} %bitcast.13, bf16[2048,2048]{1,0:T(8,128)(2,1)} %bitcast.10, bf16[6,340,340]{2,1,0:T(8,128)(2,1)} %bitcast.11, bf16[3,112,2048]{2,1,0:T(8,128)(2,1)} %bitcast.12, s32[6,1,340]{2,1,0:T(1,128)} %bitcast.14, s32[6]{0:T(128)} %bitcast.15), custom_call_target="tpu_custom_call" | custom-call | tf_op jit(solution)/shard_map/pallas_call | solution.py:236
  25.1 0.8 %copy.10 = bf16[1,1,1,112,2048]{4,3,2,1,0:T(8,128)(2,1)} copy(bf16[1,1,1,112,2048]{4,3,2,1,0:T(8,128)(2,1)S(1)} %bitcast.9) | data formatting | bytes 917504
  25.8 1.1 %copy.11 = bf16[1,1,1,6,340,340]{5,4,3,2,1,0:T(8,128)(2,1)} copy(bf16[1,1,1,6,340,340]{5,4,3,2,1,0:T(8,128)(2,1)S(1)} %bitcast.8) | data formatting | bytes 2774400
where the time goes:
time: 27.1 us; the launch traced here: 27 us
  Pallas kernels  24.4 us (90%)
  local copies, waits for them, and re-layouts  1.92 us (7%)
  between operations  0.64 us (2%)
    pallas_call x1, Pallas kernels, local(): pl.pallas_call(functools.partial(kernel, width), out_shape=(jax.ShapeDtyp...  24.4 us
    unnamed x2, local copies, waits for them, and re-layouts  1.92 us

commit v1 on v0

v1 whole, which is shorter than its diff:
```python
import functools
import math

import jax
import jax.numpy as jnp
from jax import lax
from jax.experimental import pallas as pl
from jax.experimental.pallas import tpu as pltpu
from jax.sharding import PartitionSpec as P

LANES = 128
BLOCK = 256
AXES = ("gx", "gy", "gz")
BF16, F32 = jnp.bfloat16, jnp.float32
PAIRS = ((0, 1), (2, 3), (4, 5))
X, Y, Z = PAIRS


def up(value, step):
    return -(-value // step) * step


def dot(left, right):
    return jnp.dot(left, right, preferred_element_type=F32)


def span_of(width, face):
    base = face * width // LANES * LANES
    shift = face * width - base
    return base, shift, up(shift + width, LANES)


def widest(width):
    return max(span_of(width, face)[2] for face in range(6))


def take_face(value, shift, pad):
    if shift:
        value = pltpu.roll(value, value.shape[1] - shift, 1)
    return value[:, :pad].astype(BF16)


def segments(width, start, stop):
    edges = {start, stop}
    for face in range(6):
        base, _, extent = span_of(width, face)
        edges.update(edge for edge in (base, base + extent) if start < edge < stop)
    edges = sorted(edges)
    for low, high in zip(edges[:-1], edges[1:]):
        faces = []
        for face in range(6):
            base, _, extent = span_of(width, face)
            if base <= low and high <= base + extent:
                faces.append(face)
        yield low, high, faces


def add_faces(width, value, fresh, low, high, faces):
    for face in faces:
        base = span_of(width, face)[0]
        value = value + fresh[face][:, low - base : high - base]
    return value


def outer(mapped, stored):
    return lax.dot_general(
        mapped, stored, (((0,), (0,)), ((), ())), preferred_element_type=F32
    )


def exchange(
    width, seed_hbm, op_hbm, m_hbm, saved_hbm, map_hbm, flag_hbm,
    base_ref, inp_ref, sel_v, w_v, last_ref, g_v,
    seed_v, op_v, m_v, saved_v, map_v, flag_v, send_v, recv_v, old_v, mapped_v, packed_v,
    hid_v, stb_v, wide_v, in_sem, send_sem, recv_sem,
):
    columns, trace = seed_v.shape
    sweeps = saved_v.shape[0]
    pad = up(width, LANES)
    span = 6 * width
    x_end = up(2 * width, BLOCK)
    z_start = (4 * width) // BLOCK * BLOCK
    z_only = up(4 * width, BLOCK)
    tail = trace - LANES
    chunks = ((z_start, trace), (0, x_end), (x_end, z_start))

    where = [lax.axis_index(name) for name in AXES]
    has = []
    for axis, name in enumerate(AXES):
        has.append(where[axis] > 0)
        has.append(where[axis] < lax.axis_size(name) - 1)

    def peer(face):
        return {AXES[face // 2]: where[face // 2] + (1 if face % 2 else -1)}

    seed_in = pltpu.make_async_copy(seed_hbm, seed_v, in_sem.at[0])
    seed_in.start()
    op_in = []
    for number, (start, stop) in enumerate(chunks):
        copy = pltpu.make_async_copy(
            op_hbm.at[:, start:stop], op_v.at[:, start:stop], in_sem.at[1 + number]
        )
        copy.start()
        op_in.append(copy)
    flag_in = pltpu.make_async_copy(flag_hbm, flag_v, in_sem.at[7])
    flag_in.start()
    map_in = pltpu.make_async_copy(map_hbm, map_v, in_sem.at[6])
    map_in.start()
    m_in = pltpu.make_async_copy(m_hbm, m_v, in_sem.at[4])
    m_in.start()
    saved_in = pltpu.make_async_copy(saved_hbm, saved_v, in_sem.at[5])
    saved_in.start()

    barrier = pltpu.get_barrier_semaphore()
    count = 0
    for face in range(6):
        @pl.when(has[face])
        def _(face=face):
            pl.semaphore_signal(
                barrier, inc=1, device_id=peer(face), device_id_type=pl.DeviceIdType.MESH
            )
        count = count + has[face].astype(jnp.int32)

    for face in range(6):
        @pl.when(jnp.logical_not(has[face]))
        def _(face=face):
            for sweep in range(sweeps):
                recv_v[sweep, face] = jnp.zeros((columns, pad), BF16)

    def remote(sweep, face):
        return pltpu.make_async_remote_copy(
            src_ref=send_v.at[sweep, face],
            dst_ref=recv_v.at[sweep, face ^ 1],
            send_sem=send_sem.at[sweep, face],
            recv_sem=recv_sem.at[sweep, face ^ 1],
            device_id=peer(face),
            device_id_type=pl.DeviceIdType.MESH,
        )

    def arrival(sweep, face):
        return pltpu.make_async_remote_copy(
            src_ref=send_v.at[sweep, face],
            dst_ref=recv_v.at[sweep, face],
            send_sem=send_sem.at[sweep, face],
            recv_sem=recv_sem.at[sweep, face],
            device_id=peer(face),
            device_id_type=pl.DeviceIdType.MESH,
        )

    def emit(sweep, faces, value, start):
        for face in faces:
            base, shift, extent = span_of(width, face)
            send_v[sweep, face] = take_face(
                value[:, base - start : base - start + extent], shift, pad
            )
        for face in faces:
            @pl.when(has[face])
            def _(face=face):
                remote(sweep, face).start()

    def wait_for(sweep, faces):
        for face in faces:
            @pl.when(has[face])
            def _(face=face):
                arrival(sweep, face).wait_recv()

    def take(sweep, faces):
        found = {}
        for face in faces:
            inputs = lax.select(flag_v[face] == 1, send_v[sweep, face], recv_v[sweep, face])
            if sweep == sweeps - 1:
                inp_ref[face] = inputs
            else:
                old_v[sweep, face] = inputs
                extent = span_of(width, face)[2]
                found[face] = dot(inputs, w_v[face, :, 0:extent])
        return found

    def settle(fresh, start, stop):
        for low, high, faces in segments(width, start, stop):
            value = seed_v[:, low:high].astype(F32)
            value = add_faces(width, value, fresh, low, high, faces)
            if high > tail:
                cut = max(low, tail)
                place = lax.broadcasted_iota(jnp.int32, (columns, high - cut), 1) + cut
                inner = hid_v[:, cut:high].astype(BF16).astype(F32)
                inner = jnp.where(place >= span, inner, 0.0)
                end = value[:, cut - low :] + inner
                value = end if cut == low else jnp.concatenate([value[:, : cut - low], end], axis=1)
            stb_v[:, low:high] = value.astype(BF16)

    def map_inputs(sweep):
        for face in range(6):
            mapped_v[face, sweep * columns : (sweep + 1) * columns, :] = dot(
                old_v[sweep, face], sel_v[face]
            ).astype(BF16)

    def build_maps():
        flag_in.wait()
        map_in.wait()
        rows = lax.broadcasted_iota(jnp.int32, (pad, width), 0).astype(jnp.int16)
        lane = lax.broadcasted_iota(jnp.int32, (1, width), 1)
        for face in range(6):
            flag = (flag_v[face] == 1).astype(jnp.int32)
            row = map_v[face]
            row = row + (lane - row) * flag
            sel_v[face, :, width:pad] = jnp.zeros((pad, pad - width), BF16)
            sel_v[face, :, 0:width] = jnp.where(
                rows == row.astype(jnp.int16), jnp.bfloat16(1.0), jnp.bfloat16(0.0)
            )
        m_in.wait()
        for slot in range(2):
            wide_v[slot, :, pad - LANES :] = jnp.zeros(
                (pad, wide_v.shape[2] - pad + LANES), F32
            )
        for face in range(6):
            _, shift, extent = span_of(width, face)
            wide_v[face % 2, :, 0:width] = dot(sel_v[face, :, 0:width], m_v[face])
            value = wide_v[face % 2, :, 0:extent]
            if shift:
                value = pltpu.roll(value, shift, 1)
            w_v[face, :, 0:extent] = value.astype(BF16)

    def pack():
        saved_in.wait()
        for face in range(6):
            base, shift, extent = span_of(width, face)
            for step in range(sweeps):
                value = take_face(
                    saved_v[sweeps - 1 - step, :, base : base + extent].astype(F32), shift, pad
                )
                if step == sweeps - 1:
                    last_ref[face] = value
                else:
                    packed_v[face, step * columns : (step + 1) * columns, :] = value

    y_low = span_of(width, 2)[0]
    y_high = span_of(width, 3)[0] + span_of(width, 3)[2]

    def send_all(sweep, hidden_of):
        value = hidden_of(0)
        if sweep == 0:
            pl.semaphore_wait(barrier, count)
        emit(sweep, Z, value, z_start)
        hid_v[:, z_start:y_high] = value[:, : y_high - z_start]
        hid_v[:, tail:trace] = value[:, tail - z_start :]
        value = hidden_of(1)
        emit(sweep, X, value, 0)
        hid_v[:, y_low:x_end] = value[:, y_low:]
        value = hidden_of(2)
        value = jnp.concatenate([hid_v[:, y_low:x_end], value, hid_v[:, z_start:y_high]], axis=1)
        emit(sweep, Y, value, y_low)

    seed_in.wait()

    def first(number):
        start, stop = chunks[number]
        op_in[number].wait()
        return dot(seed_v[...], op_v[:, start:stop])

    send_all(0, first)
    build_maps()
    for sweep in range(sweeps - 1):
        wait_for(sweep, Z)
        fresh = take(sweep, Z)
        settle(fresh, z_only, trace)
        ahead = dot(stb_v[:, z_only:trace], op_v[z_only:trace, z_start:trace])
        wait_for(sweep, X)
        wait_for(sweep, Y)
        fresh.update(take(sweep, X))
        fresh.update(take(sweep, Y))
        settle(fresh, 0, z_only)

        def later(number, ahead=ahead):
            start, stop = chunks[number]
            if number == 0:
                return ahead + dot(stb_v[:, 0:z_only], op_v[0:z_only, start:stop])
            return dot(stb_v[...], op_v[:, start:stop])

        send_all(sweep + 1, later)
        if sweep == 0:
            pack()
        map_inputs(sweep)

    for face in range(6):
        g_v[face] = outer(mapped_v[face], packed_v[face])
    base_ref[...] = seed_v[...].astype(F32)
    inner = hid_v[:, tail:trace].astype(BF16).astype(F32)
    place = lax.broadcasted_iota(jnp.int32, (columns, LANES), 1) + tail
    base_ref[:, tail:trace] += jnp.where(place >= span, inner, 0.0)
    for faces in (Z, X, Y):
        wait_for(sweeps - 1, faces)
        take(sweeps - 1, faces)
    for sweep in range(sweeps):
        for face in range(6):
            @pl.when(has[face])
            def _(face=face, sweep=sweep):
                remote(sweep, face).wait_send()


def finish(
    width, base_ref, inp_ref, sel_ref, w_ref, last_ref, g_ref, adjoint_hbm, gradient_hbm,
    adjoint_v, gradient_v, out_sem,
):
    columns, trace = base_ref.shape
    scale = 1.0 / math.sqrt(columns)
    fresh = {}
    for face in range(6):
        fresh[face] = dot(inp_ref[face], w_ref[face, :, 0 : span_of(width, face)[2]])
    for low, high, faces in segments(width, 0, trace):
        value = add_faces(width, base_ref[:, low:high], fresh, low, high, faces)
        adjoint_v[:, low:high] = value.astype(BF16)
    copies = [pltpu.make_async_copy(adjoint_v, adjoint_hbm, out_sem.at[6])]
    copies[0].start()
    for face in range(6):
        mapped = dot(inp_ref[face], sel_ref[face]).astype(BF16)
        total = g_ref[face] + outer(mapped, last_ref[face])
        gradient_v[face] = (total * scale).astype(BF16)[0:width, 0:width]
        copy = pltpu.make_async_copy(gradient_v.at[face], gradient_hbm.at[face], out_sem.at[face])
        copy.start()
        copies.append(copy)
    for copy in copies:
        copy.wait()


def local(seed_cotangent, trace_operator, face_matrices, saved_traces, edge_flags, node_map):
    seed, operator, matrices, stored, flags, mapping = (
        array.reshape(array.shape[3:])
        for array in (
            seed_cotangent, trace_operator, face_matrices, saved_traces, edge_flags, node_map
        )
    )
    width = matrices.shape[-1]
    sweeps, columns, trace = stored.shape
    pad = up(width, LANES)
    wide = widest(width)
    anywhere = pl.BlockSpec(memory_space=pltpu.HBM)
    resident = pl.BlockSpec(memory_space=pltpu.VMEM)
    between = pl.pallas_call(
        functools.partial(exchange, width),
        out_shape=(
            jax.ShapeDtypeStruct(seed.shape, F32),
            jax.ShapeDtypeStruct((6, columns, pad), BF16),
            jax.ShapeDtypeStruct((6, pad, pad), BF16),
            jax.ShapeDtypeStruct((6, pad, wide), BF16),
            jax.ShapeDtypeStruct((6, columns, pad), BF16),
            jax.ShapeDtypeStruct((6, pad, pad), F32),
        ),
        in_specs=[anywhere] * 6,
        out_specs=(resident,) * 6,
        scratch_shapes=[
            pltpu.VMEM(seed.shape, BF16),
            pltpu.VMEM(operator.shape, BF16),
            pltpu.VMEM(matrices.shape, BF16),
            pltpu.VMEM(stored.shape, BF16),
            pltpu.VMEM((6, 1, width), jnp.int32),
            pltpu.SMEM(flags.shape, jnp.int32),
            pltpu.VMEM((sweeps, 6, columns, pad), BF16),
            pltpu.VMEM((sweeps, 6, columns, pad), BF16),
            pltpu.VMEM((sweeps - 1, 6, columns, pad), BF16),
            pltpu.VMEM((6, (sweeps - 1) * columns, pad), BF16),
            pltpu.VMEM((6, (sweeps - 1) * columns, pad), BF16),
            pltpu.VMEM(seed.shape, F32),
            pltpu.VMEM(seed.shape, BF16),
            pltpu.VMEM((2, pad, wide), F32),
            pltpu.SemaphoreType.DMA((8,)),
            pltpu.SemaphoreType.DMA((sweeps, 6)),
            pltpu.SemaphoreType.DMA((sweeps, 6)),
        ],
        compiler_params=pltpu.CompilerParams(
            collective_id=0, has_side_effects=True, vmem_limit_bytes=40 * 1024 * 1024
        ),
    )(*(pltpu.with_memory_space_constraint(array, pltpu.HBM) for array in (seed, operator, matrices, stored, mapping[:, None, :], flags)))
    adjoint, gradient = pl.pallas_call(
        functools.partial(finish, width),
        out_shape=(
            jax.ShapeDtypeStruct(seed.shape, BF16),
            jax.ShapeDtypeStruct(matrices.shape, BF16),
        ),
        in_specs=[resident] * 6,
        out_specs=(anywhere, anywhere),
        scratch_shapes=[
            pltpu.VMEM(seed.shape, BF16),
            pltpu.VMEM(matrices.shape, BF16),
            pltpu.SemaphoreType.DMA((7,)),
        ],
        compiler_params=pltpu.CompilerParams(vmem_limit_bytes=12 * 1024 * 1024),
    )(*between)
    return adjoint[None, None, None], gradient[None, None, None]


def solution(mesh):
    return jax.shard_map(
        local,
        mesh=mesh,
        in_specs=(
            P("gx", "gy", "gz", None, None),
            P("gx", "gy", "gz", None, None),
            P("gx", "gy", "gz", None, None, None),
            P("gx", "gy", "gz", None, None, None),
            P("gx", "gy", "gz", None),
            P("gx", "gy", "gz", None, None),
        ),
        out_specs=(P("gx", "gy", "gz", None, None), P("gx", "gy", "gz", None, None, None)),
        check_vma=False,
    )
```

time: 27.1 us -> 25.6 us (0.945)
  the two profiles are of different devices: /device:TPU:1 before, /device:TPU:0 now
where the time goes in v1:
time: 25.6 us; the launch traced here: 25.4 us
  Pallas kernels  24.8 us (97%)
  between operations  0.64 us (2%)
    pallas_call x1, Pallas kernels, local(): pl.pallas_call(functools.partial(exchange, width), out_shape=(jax.ShapeDt...  21.7 us
    pallas_call x1, Pallas kernels, local(): pl.pallas_call(functools.partial(finish, width), out_shape=(jax.ShapeDtyp...  3.08 us

profile of v1, /device:TPU:0, one launch (start us, length us, event | category | flops | bytes accessed | tf_op | source)
XLA Modules:
  0.0 25.4 jit_solution(10908620281428497121)
XLA Ops:
  0.6 21.7 %shard_map.77 = (f32[112,2048]{1,0:T(8,128)S(1)}, bf16[6,112,384]{2,1,0:T(8,128)(2,1)S(1)}, bf16[6,384,384]{2,1,0:T(8,128)(2,1)S(1)}, bf16[6,384,512]{2,1,0:T(8,...) custom-call(bf16[112,2048]{1,0:T(8,128)(2,1)} %bitcast.11, bf16[2048,2048]{1,0:T(8,128)(2,1)} %bitcast.8, ...), custom_call_target="tpu_custom_call" | custom-call | tf_op jit(solution)/shard_map/pallas_call | solution.py:339
  22.3 3.1 %shard_map.78 = (bf16[112,2048]{1,0:T(8,128)(2,1)}, bf16[6,340,340]{2,1,0:T(8,128)(2,1)}) custom-call(f32[112,2048]{1,0:T(8,128)S(1)} %get-tuple-element.10.base_ref, bf16[6,112,384]{2,1,0:T(8,128)(2,1)S(1)} %get-tuple-element.11.inp_ref, bf16[6,384,384]{2,1,0:T(8,128)(2,1)S(1)} %get-tuple-element.12.sel_ref, ...), custom_call_target="tpu_custom_call" | custom-call | tf_op jit(solution)/shard_map/pallas_call | solution.py:374

commit v2 on v1

--- a/solution.py
+++ b/solution.py
@@ -10,6 +10,7 @@
 
 LANES = 128
 BLOCK = 256
+AHEAD = 2
 AXES = ("gx", "gy", "gz")
 BF16, F32 = jnp.bfloat16, jnp.float32
 PAIRS = ((0, 1), (2, 3), (4, 5))
@@ -28,6 +29,42 @@
     base = face * width // LANES * LANES
     shift = face * width - base
     return base, shift, up(shift + width, LANES)
+
+
+def groups_of(width, trace):
+    tiles = trace // BLOCK
+    z_tile = 4 * width // BLOCK
+    x_tile = up(2 * width, BLOCK) // BLOCK
+    order = list(range(tiles - 1, z_tile - 1, -1))
+    order += list(range(x_tile)) + list(range(x_tile, z_tile))
+    groups, done, sent = [], set(), set()
+    for first in range(0, tiles, 2):
+        group = sorted(order[first : first + 2])
+        done.update(group)
+        faces = []
+        for face in (5, 4, 0, 1, 2, 3):
+            base, _, extent = span_of(width, face)
+            needs = range(base // BLOCK, up(base + extent, BLOCK) // BLOCK)
+            if face not in sent and done.issuperset(needs):
+                faces.append(face)
+        sent.update(faces)
+        groups.append((group, faces))
+    return groups
+
+
+def runs_of(group):
+    runs = []
+    for tile in group:
+        if runs and runs[-1][1] == tile * BLOCK:
+            runs[-1] = (runs[-1][0], (tile + 1) * BLOCK)
+        else:
+            runs.append((tile * BLOCK, (tile + 1) * BLOCK))
+    return runs
+
+
+def gather(ref, low, high, runs):
+    parts = [ref[low:high, start:stop] for start, stop in runs]
+    return parts[0] if len(parts) == 1 else jnp.concatenate(parts, axis=1)
 
 
 def widest(width):
@@ -68,21 +105,26 @@
     )
 
 
+def scaled(width, mapped, total, stored, columns):
+    total = total + outer(mapped, stored)
+    return (total * (1.0 / math.sqrt(columns))).astype(BF16)[0:width, 0:width]
+
+
 def exchange(
     width, seed_hbm, op_hbm, m_hbm, saved_hbm, map_hbm, flag_hbm,
-    base_ref, inp_ref, sel_v, w_v, last_ref, g_v,
+    base_ref, inp_ref, given_ref, sel_v, w_v, last_ref, g_v,
     seed_v, op_v, m_v, saved_v, map_v, flag_v, send_v, recv_v, old_v, mapped_v, packed_v,
-    hid_v, stb_v, wide_v, in_sem, send_sem, recv_sem,
+    hid_v, stb_v, wide_v, in_sem, op_sem, send_sem, recv_sem,
 ):
     columns, trace = seed_v.shape
     sweeps = saved_v.shape[0]
     pad = up(width, LANES)
     span = 6 * width
-    x_end = up(2 * width, BLOCK)
-    z_start = (4 * width) // BLOCK * BLOCK
+    x_only = 2 * width // BLOCK * BLOCK
     z_only = up(4 * width, BLOCK)
     tail = trace - LANES
-    chunks = ((z_start, trace), (0, x_end), (x_end, z_start))
+    groups = groups_of(width, trace)
+    runs = [runs_of(group) for group, _ in groups]
 
     where = [lax.axis_index(name) for name in AXES]
     has = []
@@ -96,20 +138,21 @@
     seed_in = pltpu.make_async_copy(seed_hbm, seed_v, in_sem.at[0])
     seed_in.start()
     op_in = []
-    for number, (start, stop) in enumerate(chunks):
-        copy = pltpu.make_async_copy(
-            op_hbm.at[:, start:stop], op_v.at[:, start:stop], in_sem.at[1 + number]
-        )
-        copy.start()
-        op_in.append(copy)
-    flag_in = pltpu.make_async_copy(flag_hbm, flag_v, in_sem.at[7])
+    for number, group in enumerate(runs):
+        copies = []
+        for part, (start, stop) in enumerate(group):
+            copy = pltpu.make_async_copy(
+                op_hbm.at[:, start:stop], op_v.at[:, start:stop], op_sem.at[number, part]
+            )
+            copy.start()
+            copies.append(copy)
+        op_in.append(copies)
+    flag_in = pltpu.make_async_copy(flag_hbm, flag_v, in_sem.at[1])
     flag_in.start()
-    map_in = pltpu.make_async_copy(map_hbm, map_v, in_sem.at[6])
+    map_in = pltpu.make_async_copy(map_hbm, map_v, in_sem.at[2])
     map_in.start()
-    m_in = pltpu.make_async_copy(m_hbm, m_v, in_sem.at[4])
-    m_in.start()
-    saved_in = pltpu.make_async_copy(saved_hbm, saved_v, in_sem.at[5])
-    saved_in.start()
+    m_in = pltpu.make_async_copy(m_hbm, m_v, in_sem.at[3])
+    saved_in = pltpu.make_async_copy(saved_hbm, saved_v, in_sem.at[4])
 
     barrier = pltpu.get_barrier_semaphore()
     count = 0
@@ -147,16 +190,23 @@
             device_id_type=pl.DeviceIdType.MESH,
         )
 
-    def emit(sweep, faces, value, start):
+    def fill(sweep, faces):
         for face in faces:
             base, shift, extent = span_of(width, face)
-            send_v[sweep, face] = take_face(
-                value[:, base - start : base - start + extent], shift, pad
-            )
+            send_v[sweep, face] = take_face(hid_v[:, base : base + extent], shift, pad)
+
+    def launch(sweep, faces):
         for face in faces:
             @pl.when(has[face])
             def _(face=face):
                 remote(sweep, face).start()
+
+    def put(number, value, more):
+        at = 0
+        for start, stop in runs[number]:
+            piece = value[:, at : at + stop - start]
+            hid_v[:, start:stop] = hid_v[:, start:stop] + piece if more else piece
+            at += stop - start
 
     def wait_for(sweep, faces):
         for face in faces:
@@ -234,50 +284,45 @@
                 else:
                     packed_v[face, step * columns : (step + 1) * columns, :] = value
 
-    y_low = span_of(width, 2)[0]
-    y_high = span_of(width, 3)[0] + span_of(width, 3)[2]
-
-    def send_all(sweep, hidden_of):
-        value = hidden_of(0)
-        if sweep == 0:
+    def multiply(number, low, high, more, left=stb_v):
+        put(number, dot(left[:, low:high], gather(op_v, low, high, runs[number])), more)
+
+    seed_in.wait()
+    for number, (_, faces) in enumerate(groups):
+        for copy in op_in[number]:
+            copy.wait()
+        multiply(number, 0, trace, False, seed_v)
+        fill(0, faces)
+        if number == 0:
             pl.semaphore_wait(barrier, count)
-        emit(sweep, Z, value, z_start)
-        hid_v[:, z_start:y_high] = value[:, : y_high - z_start]
-        hid_v[:, tail:trace] = value[:, tail - z_start :]
-        value = hidden_of(1)
-        emit(sweep, X, value, 0)
-        hid_v[:, y_low:x_end] = value[:, y_low:]
-        value = hidden_of(2)
-        value = jnp.concatenate([hid_v[:, y_low:x_end], value, hid_v[:, z_start:y_high]], axis=1)
-        emit(sweep, Y, value, y_low)
-
-    seed_in.wait()
-
-    def first(number):
-        start, stop = chunks[number]
-        op_in[number].wait()
-        return dot(seed_v[...], op_v[:, start:stop])
-
-    send_all(0, first)
+        launch(0, faces)
+    m_in.start()
+    saved_in.start()
     build_maps()
+    half = up(trace // 2, BLOCK)
     for sweep in range(sweeps - 1):
         wait_for(sweep, Z)
         fresh = take(sweep, Z)
         settle(fresh, z_only, trace)
-        ahead = dot(stb_v[:, z_only:trace], op_v[z_only:trace, z_start:trace])
         wait_for(sweep, X)
+        fresh.update(take(sweep, X))
+        for number in range(AHEAD):
+            multiply(number, z_only, trace, False)
+        settle(fresh, 0, x_only)
         wait_for(sweep, Y)
-        fresh.update(take(sweep, X))
         fresh.update(take(sweep, Y))
-        settle(fresh, 0, z_only)
-
-        def later(number, ahead=ahead):
-            start, stop = chunks[number]
-            if number == 0:
-                return ahead + dot(stb_v[:, 0:z_only], op_v[0:z_only, start:stop])
-            return dot(stb_v[...], op_v[:, start:stop])
-
-        send_all(sweep + 1, later)
+        multiply(0, 0, x_only, True)
+        settle(fresh, x_only, z_only)
+        multiply(0, x_only, z_only, True)
+        for number, (_, faces) in enumerate(groups):
+            following = number + 1
+            ahead = following < AHEAD
+            if following < len(groups):
+                multiply(following, 0, half, ahead)
+            fill(sweep + 1, faces)
+            launch(sweep + 1, faces)
+            if following < len(groups):
+                multiply(following, half, z_only if ahead else trace, True)
         if sweep == 0:
             pack()
         map_inputs(sweep)
@@ -288,9 +333,13 @@
     inner = hid_v[:, tail:trace].astype(BF16).astype(F32)
     place = lax.broadcasted_iota(jnp.int32, (columns, LANES), 1) + tail
     base_ref[:, tail:trace] += jnp.where(place >= span, inner, 0.0)
-    for faces in (Z, X, Y):
-        wait_for(sweeps - 1, faces)
-        take(sweeps - 1, faces)
+    for pair in (Z, X):
+        wait_for(sweeps - 1, pair)
+        take(sweeps - 1, pair)
+        for face in pair:
+            given_ref[face] = dot(inp_ref[face], sel_v[face]).astype(BF16)
+    wait_for(sweeps - 1, Y)
+    take(sweeps - 1, Y)
     for sweep in range(sweeps):
         for face in range(6):
             @pl.when(has[face])
@@ -299,26 +348,35 @@
 
 
 def finish(
-    width, base_ref, inp_ref, sel_ref, w_ref, last_ref, g_ref, adjoint_hbm, gradient_hbm,
-    adjoint_v, gradient_v, out_sem,
+    width, base_ref, inp_ref, given_ref, sel_ref, w_ref, last_ref, g_ref,
+    adjoint_hbm, gradient_hbm, adjoint_v, gradient_v, mapped_v, out_sem,
 ):
     columns, trace = base_ref.shape
-    scale = 1.0 / math.sqrt(columns)
+    copies = []
+
+    def write(source, target):
+        copy = pltpu.make_async_copy(source, target, out_sem.at[len(copies)])
+        copy.start()
+        copies.append(copy)
+
+    def grade(faces, mapped):
+        for face in faces:
+            gradient_v[face] = scaled(width, mapped[face][...], g_ref[face], last_ref[face], columns)
+        part = slice(faces[0], faces[-1] + 1)
+        write(gradient_v.at[part], gradient_hbm.at[part])
+
+    for face in Y:
+        mapped_v[face - Y[0]] = dot(inp_ref[face], sel_ref[face]).astype(BF16)
+    grade(Z, given_ref)
+    grade(X, given_ref)
     fresh = {}
     for face in range(6):
         fresh[face] = dot(inp_ref[face], w_ref[face, :, 0 : span_of(width, face)[2]])
     for low, high, faces in segments(width, 0, trace):
         value = add_faces(width, base_ref[:, low:high], fresh, low, high, faces)
         adjoint_v[:, low:high] = value.astype(BF16)
-    copies = [pltpu.make_async_copy(adjoint_v, adjoint_hbm, out_sem.at[6])]
-    copies[0].start()
-    for face in range(6):
-        mapped = dot(inp_ref[face], sel_ref[face]).astype(BF16)
-        total = g_ref[face] + outer(mapped, last_ref[face])
-        gradient_v[face] = (total * scale).astype(BF16)[0:width, 0:width]
-        copy = pltpu.make_async_copy(gradient_v.at[face], gradient_hbm.at[face], out_sem.at[face])
-        copy.start()
-        copies.append(copy)
+    write(adjoint_v, adjoint_hbm)
+    grade(Y, [None, None, mapped_v.at[0], mapped_v.at[1]])
     for copy in copies:
         copy.wait()
 
@@ -341,13 +399,14 @@
         out_shape=(
             jax.ShapeDtypeStruct(seed.shape, F32),
             jax.ShapeDtypeStruct((6, columns, pad), BF16),
+            jax.ShapeDtypeStruct((6, columns, pad), BF16),
             jax.ShapeDtypeStruct((6, pad, pad), BF16),
             jax.ShapeDtypeStruct((6, pad, wide), BF16),
             jax.ShapeDtypeStruct((6, columns, pad), BF16),
             jax.ShapeDtypeStruct((6, pad, pad), F32),
         ),
         in_specs=[anywhere] * 6,
-        out_specs=(resident,) * 6,
+        out_specs=(resident,) * 7,
         scratch_shapes=[
             pltpu.VMEM(seed.shape, BF16),
             pltpu.VMEM(operator.shape, BF16),
@@ -363,7 +422,8 @@
             pltpu.VMEM(seed.shape, F32),
             pltpu.VMEM(seed.shape, BF16),
             pltpu.VMEM((2, pad, wide), F32),
-            pltpu.SemaphoreType.DMA((8,)),
+            pltpu.SemaphoreType.DMA((5,)),
+            pltpu.SemaphoreType.DMA((trace // BLOCK // 2, 2)),
             pltpu.SemaphoreType.DMA((sweeps, 6)),
             pltpu.SemaphoreType.DMA((sweeps, 6)),
         ],
@@ -377,12 +437,13 @@
             jax.ShapeDtypeStruct(seed.shape, BF16),
             jax.ShapeDtypeStruct(matrices.shape, BF16),
         ),
-        in_specs=[resident] * 6,
+        in_specs=[resident] * 7,
         out_specs=(anywhere, anywhere),
         scratch_shapes=[
             pltpu.VMEM(seed.shape, BF16),
             pltpu.VMEM(matrices.shape, BF16),
-            pltpu.SemaphoreType.DMA((7,)),
+            pltpu.VMEM((2, columns, pad), BF16),
+            pltpu.SemaphoreType.DMA((4,)),
         ],
         compiler_params=pltpu.CompilerParams(vmem_limit_bytes=12 * 1024 * 1024),
     )(*between)

time: 25.6 us -> 24 us (0.938)
  Pallas kernels: 24.8 us -> 23.2 us
    pallas_call x1, Pallas kernels: 3.08 us -> 1.96 us  [local(): pl.pallas_call(functools.partial(finish, width), out_shape=(jax.ShapeDtyp...]
    pallas_call x1, Pallas kernels: 21.7 us -> 21.3 us  [local(): pl.pallas_call(functools.partial(exchange, width), out_shape=(jax.ShapeDt...]
where the time goes in v2:
time: 24 us; the launch traced here: 23.9 us
  Pallas kernels  23.2 us (97%)
  between operations  0.64 us (3%)
    pallas_call x1, Pallas kernels, local(): pl.pallas_call(functools.partial(exchange, width), out_shape=(jax.ShapeDt...  21.3 us
    pallas_call x1, Pallas kernels, local(): pl.pallas_call(functools.partial(finish, width), out_shape=(jax.ShapeDtyp...  1.96 us

profile of v2, /device:TPU:0, one launch (start us, length us, event | category | flops | bytes accessed | tf_op | source)
XLA Modules:
  0.0 23.9 jit_solution(12460323251527321395)
XLA Ops:
  0.6 21.3 %shard_map.77 = (f32[112,2048]{1,0:T(8,128)S(1)}, bf16[6,112,384]{2,1,0:T(8,128)(2,1)S(1)}, bf16[6,112,384]{2,1,0:T(8,128)(2,1)S(1)}, bf16[6,384,384]{2,1,0:T(8,...) custom-call(bf16[112,2048]{1,0:T(8,128)(2,1)} %bitcast.11, ...), custom_call_target="tpu_custom_call" | custom-call | tf_op jit(solution)/shard_map/pallas_call | solution.py:397
  21.9 2.0 %shard_map.78 = (bf16[112,2048]{1,0:T(8,128)(2,1)}, bf16[6,340,340]{2,1,0:T(8,128)(2,1)}) custom-call(f32[112,2048]{1,0:T(8,128)S(1)} %get-tuple-element.11.base_ref, bf16[6,112,384]{2,1,0:T(8,128)(2,1)S(1)} %get-tuple-element.12.inp_ref, bf16[6,112,384]{2,1,0:T(8,128)(2,1)S(1)} %get-tuple-element.13.given_ref, ...), custom_call_target="tpu_custom_call" | custom-call | tf_op jit(solution)/shard_map/pallas_call | solution.py:434

commit v3 on v2

--- a/solution.py
+++ b/solution.py
@@ -33,16 +33,14 @@
 
 def groups_of(width, trace):
     tiles = trace // BLOCK
-    z_tile = 4 * width // BLOCK
-    x_tile = up(2 * width, BLOCK) // BLOCK
-    order = list(range(tiles - 1, z_tile - 1, -1))
-    order += list(range(x_tile)) + list(range(x_tile, z_tile))
+    order = list(range(4 * width // BLOCK, up(5 * width, BLOCK) // BLOCK))
+    order += [tile for tile in range(tiles) if tile not in order]
     groups, done, sent = [], set(), set()
     for first in range(0, tiles, 2):
         group = sorted(order[first : first + 2])
         done.update(group)
         faces = []
-        for face in (5, 4, 0, 1, 2, 3):
+        for face in (4, 0, 2, 1, 5, 3):
             base, _, extent = span_of(width, face)
             needs = range(base // BLOCK, up(base + extent, BLOCK) // BLOCK)
             if face not in sent and done.issuperset(needs):

time: 24 us -> 23.1 us (0.963)
  Pallas kernels: 23.2 us -> 22.3 us
    pallas_call x1, Pallas kernels: 21.3 us -> 20.3 us  [local(): pl.pallas_call(functools.partial(exchange, width), out_shape=(jax.ShapeDt...]
where the time goes in v3:
time: 23.1 us; the launch traced here: 22.9 us
  Pallas kernels  22.3 us (97%)
  between operations  0.64 us (3%)
    pallas_call x1, Pallas kernels, local(): pl.pallas_call(functools.partial(exchange, width), out_shape=(jax.ShapeDt...  20.3 us
    pallas_call x1, Pallas kernels, local(): pl.pallas_call(functools.partial(finish, width), out_shape=(jax.ShapeDtyp...  1.96 us

profile of v3, /device:TPU:0, one launch (start us, length us, event | category | flops | bytes accessed | tf_op | source)
XLA Modules:
  0.0 22.9 jit_solution(13810232541924294981)
XLA Ops:
  0.6 20.3 %shard_map.77 = (f32[112,2048]{1,0:T(8,128)S(1)}, bf16[6,112,384]{2,1,0:T(8,128)(2,1)S(1)}, bf16[6,112,384]{2,1,0:T(8,128)(2,1)S(1)}, bf16[6,384,384]{2,1,0:T(8,...) custom-call(bf16[112,2048]{1,0:T(8,128)(2,1)} %bitcast.11, ...), custom_call_target="tpu_custom_call" | custom-call | tf_op jit(solution)/shard_map/pallas_call | solution.py:395
  21.0 2.0 %shard_map.78 = (bf16[112,2048]{1,0:T(8,128)(2,1)}, bf16[6,340,340]{2,1,0:T(8,128)(2,1)}) custom-call(f32[112,2048]{1,0:T(8,128)S(1)} %get-tuple-element.11.base_ref, bf16[6,112,384]{2,1,0:T(8,128)(2,1)S(1)} %get-tuple-element.12.inp_ref, bf16[6,112,384]{2,1,0:T(8,128)(2,1)S(1)} %get-tuple-element.13.given_ref, ...), custom_call_target="tpu_custom_call" | custom-call | tf_op jit(solution)/shard_map/pallas_call | solution.py:432
